TPU v7x, 32 devices: a whole 2x2x4 slice. The times are simulated.
32 devices in a mesh: index: 8 (over y, x, core), query: 4 (over z).
Axes of the slice: x: 2, y: 2, z: 4, core: 2. Of those that a mesh axis runs over, the one named last changes fastest.
Arguments:
- queries: bfloat16 [256, 2048], P(('index', 'query')), may hold values from -4 to 4
- slab: bfloat16 [131072, 2048], P(('index', 'query')), may hold values from -24 to 24
- cand_owner: int32 [256, 32], P(('index', 'query')), may hold values from 0 to 31, all different within a row; in each aligned block of 8 rows (0 to 7, 8 to 15, ...) at most 8 rows name the same one
- cand_row: int32 [256, 32], P(('index', 'query')), may hold values from 0 to 4095
Outputs:
- pooled: float32 [256, 256], P(('index', 'query'))
- coarse_lse: float32 [256], P(('index', 'query'))
- margin: float32 [256, 32], P(('index', 'query'))
Inputs may be any that keep to these rules, and one draw needn't show every extreme that they name: `cand_owner`: each query names 32 distinct owners. Over the 8 queries of one device (aligned blocks of 8 rows) no owner is named more than 8 times, a bound that some block reaches.
All inputs are finite; a program needn't handle non-finite values.
Results may differ from a plain program's by a relative error of at most 0.00165.
Values may be sent and summed in bfloat16 or wider, within the bound.
No kernel may reach another device: no remote copies, remote signals or barrier semaphores. Data moves between devices by JAX's collectives and lax.ppermute only.
A program may use at most 128 MiB of HBM per device.

v0:
```python
import jax
import jax.numpy as jnp
from jax import lax
from jax.sharding import PartitionSpec as P

PREFIX = 256


def on_device(queries, slab, cand_owner, cand_row):
    q_dev = queries.shape[0]
    width = slab.shape[1]
    owners = lax.axis_size(("index", "query"))
    k_count = cand_owner.shape[1]
    prefix_keys = slab[:, :PREFIX]
    scale = PREFIX ** (-0.5)
    logits = (
        lax.dot_general(
            lax.all_gather(queries[:, :PREFIX], ("index", "query"), axis=0, tiled=True),
            prefix_keys,
            (((1,), (1,)), ((), ())),
            preferred_element_type=jnp.float32,
        )
        * scale
    )
    top = lax.pmax(jnp.max(logits, axis=1), ("index", "query"))
    weights = jnp.exp(logits - top[:, None])
    parts = (
        jnp.dot(weights.astype(jnp.bfloat16), prefix_keys, preferred_element_type=jnp.float32),
        jnp.sum(weights, axis=1),
    )
    results = lax.psum_scatter(parts, ("index", "query"), scatter_dimension=0, tiled=True)
    pooled_sum = results[0]
    total = results[1]
    my_start = lax.axis_index(("index", "query")) * q_dev
    my_top = lax.dynamic_slice_in_dim(top, my_start, q_dev, 0)
    pooled = pooled_sum / total[:, None]
    coarse_lse = my_top + jnp.log(total)
    capacity = max(2, min(q_dev, 2 * q_dev * k_count // owners))
    flat_owner = cand_owner.reshape(-1)
    flat_row = cand_row.reshape(-1)
    hits = (flat_owner[:, None] == jnp.arange(owners, dtype=jnp.int32)[None, :]).astype(jnp.int32)
    earlier = jnp.cumsum(hits, axis=0) - hits
    slot = jnp.sum(earlier * hits, axis=1)
    target = flat_owner * capacity + slot
    request = jnp.zeros((owners * capacity,), jnp.int32).at[target].set(flat_row)
    fetched = lax.all_to_all(
        slab[
            lax.all_to_all(
                request.reshape(owners, capacity),
                ("index", "query"),
                split_axis=0,
                concat_axis=0,
                tiled=True,
            )
        ],
        ("index", "query"),
        split_axis=0,
        concat_axis=0,
        tiled=True,
    )
    cand_rows = fetched.reshape(owners * capacity, width)[target].reshape(q_dev, k_count, width)
    full = jnp.einsum(
        "qw,qkw->qk", queries, cand_rows, preferred_element_type=jnp.float32
    ) * width ** (-0.5)
    margin = full - coarse_lse[:, None]
    return (pooled, coarse_lse, margin)


def solution(mesh):
    in_specs = (
        P(("index", "query"), None),
        P(("index", "query"), None),
        P(("index", "query"), None),
        P(("index", "query"), None),
    )
    out_specs = (P(("index", "query"), None), P(("index", "query")), P(("index", "query"), None))
    return jax.shard_map(
        on_device, mesh=mesh, in_specs=in_specs, out_specs=out_specs, check_vma=False
    )
```

profile of v0, /device:TPU:0, one launch (start us, length us, event | category | flops | bytes accessed | tf_op | source)
XLA Modules:
  0.0 318.5 jit_solution(5790546167381804350)
XLA Ops:
  7.2 0.8 eq.29
  7.9 0.8 eq.25
  8.7 0.7 broadcast_multiply_fusion
  9.4 0.8 reshape.120
  10.1 0.1 mul.43
  10.2 0.6 reduce-window.6
  10.8 0.2 slice_reduce_fusion
  11.1 0.1 fusion.11
  11.2 1.4 scatter_custom_fusion
  12.6 0.1 all_to_all.11
  12.7 14.3 %all_to_all.17 = s32[32,1,8]{2,1,0:T(1,128)S(1)} all-to-all(s32[32,1,8]{2,1,0:T(1,128)S(1)} %bitcast.36), channel_id=1, replica_groups=mesh['index'=8,'query'=4] {'index','query'}, dimensions={0} | all-to-all | bytes 2048 | tf_op jit(solution)/shard_map/all_to_all | solution.py:48
  27.0 0.1 reshape.102
  27.1 0.0 slice-start
  27.1 11.3 %gather_fusion = bf16[256,2048]{1,0:T(8,128)(2,1)} fusion(bf16[4096,2048]{1,0:T(8,128)(2,1)} %param.5, s32[1024]{0:T(1024)S(1)} %pad_clamp_fusion.1), kind=kCustom, calls=%fused_computation | custom fusion | bytes 2098176 | tf_op jit(solution)/shard_map/gather | solution.py:47
  38.4 2.6 all-to-all-start.1
  41.0 0.0 reduce-scatter.2.cloned.1.call-start
  41.1 0.0 slice-done
  41.1 84.3 %all_gather.3 = bf16[256,256]{1,0:T(8,128)(2,1)S(1)} all-gather(bf16[8,256]{1,0:T(8,128)(2,1)S(1)} %slice-done), channel_id=1, replica_groups=mesh['index'=8,'query'=4] {'index','query'}, dimensions={0}, use_global_device_ids=true | all-gather | bytes 135168 | tf_op jit(solution)/shard_map/all_gather | solution.py:18
  125.4 4.3 %fusion.15 = (f32[256]{0:T(256)S(1)}, f32[256,4096]{1,0:T(8,128)}) fusion(bf16[256,256]{1,0:T(8,128)(2,1)S(1)} %all_gather.3, bf16[4096,2048]{1,0:T(8,128)(2,1)} %param.5), kind=kOutput, calls=%fused_computation.32 | convolution fusion | flops 538967808 | bytes 6423552 | tf_op jit(solution)/shard_map/dot_general | solution.py:17
  129.6 36.8 %pmax.7 = f32[256]{0:T(256)S(1)} all-reduce(f32[256]{0:T(256)S(1)} %get-tuple-element.5), channel_id=1, replica_groups=mesh['index'=8,'query'=4] {'index','query'}, use_global_device_ids=true, to_apply=%region_1.0 | all-reduce | flops 256 | bytes 2048 | tf_op jit(solution)/shard_map/pmax | solution.py:25
  166.4 4.3 %fusion.2 = f32[256,256]{1,0:T(8,128)} fusion(f32[256,4096]{1,0:T(8,128)} %get-tuple-element.6, f32[256]{0:T(256)S(1)} %pmax.7, bf16[4096,2048]{1,0:T(8,128)(2,1)} %param.5), kind=kOutput, calls=%fused_computation.7 | convolution fusion | flops 538968064 | bytes 6554624 | tf_op jit(solution)/shard_map/dot_general | solution.py:28
  170.8 0.0 reduce-scatter.2.cloned.1.call-update
  170.8 2.9 fusion
  173.7 42.3 %all-reduce = f32[256]{0:T(256)S(1)} all-reduce(f32[256]{0:T(256)S(1)} %fusion), channel_id=3, replica_groups=mesh['index'=8,'query'=4] {'index','query'}, use_global_device_ids=true, to_apply=%region_4.0.clone | all-reduce | flops 256 | bytes 2048
  216.0 0.1 log_add_fusion
  216.0 0.0 copy-start.1
  216.0 91.8 %reduce-scatter.2.cloned.1.call-done = f32[8,256]{1,0:T(8,128)} async-done(((f32[256,256]{1,0:T(8,128)}), f32[8,256]{1,0:T(8,128)}) %reduce-scatter.2.cloned.1.call-update) | async-done | bytes 8208 | tf_op jit(solution)/shard_map/reduce_scatter | solution.py:31
  307.9 1.4 broadcast_divide_fusion
  309.2 0.0 all-to-all-done.1
  309.2 0.0 copy-start
  309.3 1.4 gather_fusion.1
  310.6 0.0 copy-done
  310.6 0.4 fusion.7
  311.0 0.0 copy-done.1
  311.0 0.7 multiply_subtract_fusion
  (7 shorter events, 0.1 us)
Async XLA Ops:
  27.1 14.0 %slice-start = ((bf16[8,2048]{1,0:T(8,128)(2,1)}), bf16[8,256]{1,0:T(8,128)(2,1)S(1)}, s32[]{:S(2)}) async-start(bf16[8,2048]{1,0:T(8,128)(2,1)} %param.4), calls=%async_computation.4 | async-start | bytes 8192 | tf_op jit(solution)/shard_map/slice | solution.py:18
  38.4 270.9 %all-to-all-start.1 = ((bf16[32,8,2048]{2,1,0:T(8,128)(2,1)}), bf16[32,8,2048]{2,1,0:T(8,128)(2,1)S(1)}, u32[]{:S(2)}, u32[]{:S(2)}) async-start(bf16[32,8,2048]{2,1,0:T(8,128)(2,1)} %bitcast.5), calls=%async_computation.2 | async-start | bytes 2097152 | tf_op jit(solution)/shard_map/all_to_all | solution.py:46
  41.0 266.8 %reduce-scatter.2.cloned.1.call-start = ((), (), s32[]{:S(2)}) async-start(), calls=%async_computation.3 | async-start | bytes 270336 | tf_op jit(solution)/shard_map/reduce_scatter | solution.py:31
  216.0 95.0 %copy-start.1 = (f32[8]{0:T(128)}, f32[8]{0:T(128)S(1)}, u32[]{:S(2)}) copy-start(f32[8]{0:T(128)S(1)} %get-tuple-element.3) | copy-start | bytes 100
  309.2 1.4 copy-start
Sparse Core Ops, SparseCore 0:
  170.9 136.9 reduce-scatter.1
where the time goes:
time: 319 us
  blocking collectives  178 us (56%)
  waiting for transfers between devices  91.9 us (29%)
  local copies, waits for them, and re-layouts  16.8 us (5%)
  between operations  14.1 us (4%)
  matrix products  8.96 us (3%)
  other arithmetic  6.46 us (2%)
    reduce_scatter x1, waiting for transfers between devices, on_device(): lax.psum_scatter(parts, ('index', 'query'), scatter_dimension=0, tiled=True)  91.8 us
    all_gather x1, blocking collectives, on_device(): lax.all_gather(queries[:, :PREFIX], ('index', 'query'), axis=0, tiled=True)  84.3 us
    unnamed x1, blocking collectives  42.3 us
    pmax x1, blocking collectives, on_device(): top = lax.pmax(jnp.max(logits, axis=1), ('index', 'query'))  36.8 us
    all_to_all x1, blocking collectives, on_device(): lax.all_to_all(request.reshape(owners, capacity), ('index', 'query'), spl...  14.3 us
    gather x1, local copies, waits for them, and re-layouts, on_device(): slab[lax.all_to_all(request.reshape(owners, capacity), ('index', 'query')...  11.3 us
  transfers between devices with their start and end apart: 2, of which 1 were waited for; matrix products, arithmetic and copies ran while one was open for 4% of the time, Pallas kernels for 0%

commit v1 on v0

--- a/solution.py
+++ b/solution.py
@@ -4,6 +4,27 @@
 from jax.sharding import PartitionSpec as P
 
 PREFIX = 256
+
+
+def in_order(blocks, dim):
+    shape = list(blocks.shape[1:])
+    shape[dim] *= blocks.shape[0]
+    return jnp.moveaxis(blocks, 0, dim).reshape(shape)
+
+
+def grow_blocks(x, axis):
+    size, here = (lax.axis_size(axis), lax.axis_index(axis))
+    tiles, stride = (x[None], 1)
+    while stride < size:
+        received = lax.ppermute(tiles, axis, [(i, i ^ stride) for i in range(size)])
+        low = here & stride == 0
+        tiles = jnp.concatenate([jnp.where(low, tiles, received), jnp.where(low, received, tiles)])
+        stride *= 2
+    return tiles
+
+
+def doubled_up(x, axis, dim):
+    return in_order(grow_blocks(x, axis), dim)
 
 
 def on_device(queries, slab, cand_owner, cand_row):
@@ -15,7 +36,7 @@
     scale = PREFIX ** (-0.5)
     logits = (
         lax.dot_general(
-            lax.all_gather(queries[:, :PREFIX], ("index", "query"), axis=0, tiled=True),
+            doubled_up(queries[:, :PREFIX], ("index", "query"), 0),
             prefix_keys,
             (((1,), (1,)), ((), ())),
             preferred_element_type=jnp.float32,

time: 319 us -> 252 us (0.79)
  blocking collectives: 178 us -> 79.7 us
  waiting for transfers between devices: 91.9 us -> 109 us
  starting transfers between devices: 2.69 us -> 13.8 us
    all_gather x1 -> x0, blocking collectives: 84.3 us -> none  [on_device(): lax.all_gather(queries[:, :PREFIX], ('index', 'query'), axis=0, tiled=True)]
    all_to_all x1 -> x0, blocking collectives: 14.3 us -> none  [on_device(): lax.all_to_all(request.reshape(owners, capacity), ('index', 'query'), spl...]
    ppermute x0 -> x5, waiting for transfers between devices: none -> 9.55 us  [grow_blocks(): received = lax.ppermute(tiles, axis, [(i, i ^ stride) for i in range(size)])]
    ppermute x0 -> x5, starting transfers between devices: none -> 8.33 us  [grow_blocks(): received = lax.ppermute(tiles, axis, [(i, i ^ stride) for i in range(size)])]
    all_to_all x0 -> x1, waiting for transfers between devices: none -> 6.82 us  [on_device(): lax.all_to_all(request.reshape(owners, capacity), ('index', 'query'), spl...]
  transfers between devices with their start and end apart: 2 -> 8, of which waited for: 1 -> 3; matrix products, arithmetic and copies ran while one was open for 4% -> 12% of each run, Pallas kernels for 0% -> 0%
where the time goes in v1:
time: 252 us; the launch traced here: 251 us
  waiting for transfers between devices  109 us (43%)
  blocking collectives  79.7 us (32%)
  local copies, waits for them, and re-layouts  18 us (7%)
  between operations  14.2 us (6%)
  starting transfers between devices  13.8 us (5%)
  matrix products  8.97 us (4%)
  other arithmetic  7.23 us (3%)
    reduce_scatter x1, waiting for transfers between devices, on_device(): lax.psum_scatter(parts, ('index', 'query'), scatter_dimension=0, tiled=True)  92.4 us
    unnamed x1, blocking collectives  40.7 us
    pmax x1, blocking collectives, on_device(): top = lax.pmax(jnp.max(logits, axis=1), ('index', 'query'))  39 us
    gather x1, local copies, waits for them, and re-layouts, on_device(): slab[lax.all_to_all(request.reshape(owners, capacity), ('index', 'query')...  11.3 us
    ppermute x5, waiting for transfers between devices, grow_blocks(): received = lax.ppermute(tiles, axis, [(i, i ^ stride) for i in range(size)])  9.55 us
    ppermute x5, starting transfers between devices, grow_blocks(): received = lax.ppermute(tiles, axis, [(i, i ^ stride) for i in range(size)])  8.33 us
    all_to_all x1, waiting for transfers between devices, on_device(): lax.all_to_all(request.reshape(owners, capacity), ('index', 'query'), spl...  6.82 us
  transfers between devices with their start and end apart: 8, of which 3 were waited for; matrix products, arithmetic and copies ran while one was open for 12% of the time, Pallas kernels for 0%

profile of v1, /device:TPU:0, one launch (start us, length us, event | category | flops | bytes accessed | tf_op | source)
XLA Modules:
  0.0 250.8 jit_solution(4562514205227753045)
XLA Ops:
  7.2 0.7 slice_bitcast_fusion
  7.9 3.1 %collective-permute-start = (bf16[1,8,256]{2,1,0:T(8,128)(2,1)S(1)}, bf16[1,8,256]{2,1,0:T(8,128)(2,1)S(1)}, u32[]{:S(2)}, u32[]{:S(2)}) collective-permute-start(bf16[1,8,256]{2,1,0:T(8,128)(2,1)S(1)} %slice_bitcast_fusion), channel_id=1, source_target_pairs={{0,1},{1,0},{2,3},{3,2},{4,5},{5,4},{6,7},{7,6},{8,9},{9,8},{10,11... | collective-permute-start | bytes 12296 | tf_op jit(solution)/shard_map/ppermute | solution.py:19
  10.9 0.8 eq.49
  11.7 0.8 eq.45
  12.4 0.7 broadcast_multiply_fusion
  13.1 0.6 reduce-window.6
  13.7 0.2 slice_reduce_fusion
  13.9 0.1 fusion.13
  14.1 0.1 mul.44
  14.1 0.0 collective-permute-done
  14.1 0.7 broadcast_select_fusion.9
  14.8 2.6 %collective-permute-start.1 = (bf16[2,8,256]{2,1,0:T(8,128)(2,1)S(1)}, bf16[2,8,256]{2,1,0:T(8,128)(2,1)S(1)}, u32[]{:S(2)}, u32[]{:S(2)}) collective-permute-start(bf16[2,8,256]{2,1,0:T(8,128)(2,1)S(1)} %pad_maximum_fusion.3), channel_id=1, source_target_pairs={{0,2},{1,3},{2,0},{3,1},{4,6},{5,7},{6,4},{7,5},{8,10},{9,11},{10,... | collective-permute-start | bytes 24584 | tf_op jit(solution)/shard_map/ppermute | solution.py:19
  17.4 0.8 reshape.124
  18.2 1.4 scatter_custom_fusion
  19.6 0.7 all_to_all.11
  20.3 2.8 %all-to-all-start = ((s32[32,1,8]{2,1,0:T(1,128)}), s32[32,1,8]{2,1,0:T(1,128)S(1)}, u32[]{:S(2)}, u32[]{:S(2)}) async-start(s32[32,1,8]{2,1,0:T(1,128)} %bitcast.5), calls=%async_computation.1 | async-start | bytes 32768 | tf_op jit(solution)/shard_map/all_to_all | solution.py:69
  23.1 0.0 collective-permute-done.1
  23.2 0.3 collective-permute-start.2
  23.5 6.8 %all-to-all-done = s32[32,1,8]{2,1,0:T(1,128)S(1)} async-done(((s32[32,1,8]{2,1,0:T(1,128)}), s32[32,1,8]{2,1,0:T(1,128)S(1)}, u32[]{:S(2)}, u32[]{:S(2)}) %all-to-all-start) | async-done | bytes 1056 | tf_op jit(solution)/shard_map/all_to_all | solution.py:69
  30.3 0.1 reshape.106
  30.4 0.0 collective-permute-done.2
  30.4 0.7 collective-permute-start.3
  31.1 11.3 %gather_fusion = bf16[256,2048]{1,0:T(8,128)(2,1)} fusion(bf16[4096,2048]{1,0:T(8,128)(2,1)} %param.5, s32[1024]{0:T(1024)S(1)} %pad_clamp_fusion.1), kind=kCustom, calls=%fused_computation | custom fusion | bytes 2098176 | tf_op jit(solution)/shard_map/gather | solution.py:68
  42.4 2.6 %all-to-all-start.1 = ((bf16[32,8,2048]{2,1,0:T(8,128)(2,1)}), bf16[32,8,2048]{2,1,0:T(8,128)(2,1)S(1)}, u32[]{:S(2)}, u32[]{:S(2)}) async-start(bf16[32,8,2048]{2,1,0:T(8,128)(2,1)} %bitcast.7), calls=%async_computation.2 | async-start | bytes 2097152 | tf_op jit(solution)/shard_map/all_to_all | solution.py:67
  45.0 0.0 reduce-scatter.2.cloned.1.call-start
  45.1 0.0 collective-permute-done.3
  45.1 1.7 collective-permute-start.4
  46.8 9.5 %collective-permute-done.4 = bf16[16,8,256]{2,1,0:T(8,128)(2,1)S(1)} collective-permute-done((bf16[16,8,256]{2,1,0:T(8,128)(2,1)S(1)}, bf16[16,8,256]{2,1,0:T(8,128)(2,1)S(1)}, u32[]{:S(2)}, u32[]{:S(2)}) %collective-permute-start.4) | collective-permute-done | bytes 65568 | tf_op jit(solution)/shard_map/ppermute | solution.py:19
  56.4 4.3 %fusion.18 = (f32[256]{0:T(256)S(1)}, f32[256,4096]{1,0:T(8,128)}) fusion(bf16[4096,2048]{1,0:T(8,128)(2,1)} %param.5, bf16[16,8,256]{2,1,0:T(8,128)(2,1)S(1)} %get-tuple-element.6, bf16[16,8,256]{2,1,0:T(8,128)(2,1)S(1)} %get-tuple-element.5), kind=kOutput, calls=%fused_computation.51 | convolution fusion | flops 539033344 | bytes 6423552 | tf_op jit(solution)/shard_map/dot_general | solution.py:38
  60.6 39.0 %pmax.7 = f32[256]{0:T(256)S(1)} all-reduce(f32[256]{0:T(256)S(1)} %get-tuple-element.15), channel_id=1, replica_groups=mesh['index'=8,'query'=4] {'index','query'}, use_global_device_ids=true, to_apply=%region_1.2 | all-reduce | flops 256 | bytes 2048 | tf_op jit(solution)/shard_map/pmax | solution.py:46
  99.7 4.3 %fusion.2 = f32[256,256]{1,0:T(8,128)} fusion(f32[256,4096]{1,0:T(8,128)} %get-tuple-element.16, f32[256]{0:T(256)S(1)} %pmax.7, bf16[4096,2048]{1,0:T(8,128)(2,1)} %param.5), kind=kOutput, calls=%fused_computation.7 | convolution fusion | flops 538968064 | bytes 6554624 | tf_op jit(solution)/shard_map/dot_general | solution.py:49
  104.0 0.0 reduce-scatter.2.cloned.1.call-update
  104.1 2.9 %fusion = f32[256]{0:T(256)S(1)} fusion(f32[256,4096]{1,0:T(8,128)} %get-tuple-element.16, f32[256]{0:T(256)S(1)} %pmax.7), kind=kLoop, calls=%fused_computation.5 | loop fusion | flops 2096896 | bytes 4196352 | tf_op jit(solution)/shard_map/reduce_sum | solution.py:50
  107.0 40.7 %all-reduce = f32[256]{0:T(256)S(1)} all-reduce(f32[256]{0:T(256)S(1)} %fusion), channel_id=3, replica_groups=mesh['index'=8,'query'=4] {'index','query'}, use_global_device_ids=true, to_apply=%region_4.5.clone | all-reduce | flops 256 | bytes 2048
  147.6 0.1 log_add_fusion
  147.7 0.0 copy-start
  147.7 92.4 %reduce-scatter.2.cloned.1.call-done = f32[8,256]{1,0:T(8,128)} async-done(((f32[256,256]{1,0:T(8,128)}), f32[8,256]{1,0:T(8,128)}) %reduce-scatter.2.cloned.1.call-update) | async-done | bytes 8208 | tf_op jit(solution)/shard_map/reduce_scatter | solution.py:52
  240.2 1.4 broadcast_divide_fusion
  241.5 0.0 all-to-all-done.1
  241.5 0.0 copy-start.1
  241.5 1.4 gather_fusion.1
  242.9 0.0 copy-done.1
  242.9 0.4 fusion.9
  243.3 0.0 copy-done
  243.3 0.7 multiply_subtract_fusion
  (15 shorter events, 0.1 us)
Async XLA Ops:
  7.9 6.3 %collective-permute-start = (bf16[1,8,256]{2,1,0:T(8,128)(2,1)S(1)}, bf16[1,8,256]{2,1,0:T(8,128)(2,1)S(1)}, u32[]{:S(2)}, u32[]{:S(2)}) collective-permute-start(bf16[1,8,256]{2,1,0:T(8,128)(2,1)S(1)} %slice_bitcast_fusion), channel_id=1, source_target_pairs={{0,1},{1,0},{2,3},{3,2},{4,5},{5,4},{6,7},{7,6},{8,9},{9,8},{10,11... | collective-permute-start | bytes 12296 | tf_op jit(solution)/shard_map/ppermute | solution.py:19
  14.8 8.3 %collective-permute-start.1 = (bf16[2,8,256]{2,1,0:T(8,128)(2,1)S(1)}, bf16[2,8,256]{2,1,0:T(8,128)(2,1)S(1)}, u32[]{:S(2)}, u32[]{:S(2)}) collective-permute-start(bf16[2,8,256]{2,1,0:T(8,128)(2,1)S(1)} %pad_maximum_fusion.3), channel_id=1, source_target_pairs={{0,2},{1,3},{2,0},{3,1},{4,6},{5,7},{6,4},{7,5},{8,10},{9,11},{10,... | collective-permute-start | bytes 24584 | tf_op jit(solution)/shard_map/ppermute | solution.py:19
  20.3 10.0 %all-to-all-start = ((s32[32,1,8]{2,1,0:T(1,128)}), s32[32,1,8]{2,1,0:T(1,128)S(1)}, u32[]{:S(2)}, u32[]{:S(2)}) async-start(s32[32,1,8]{2,1,0:T(1,128)} %bitcast.5), calls=%async_computation.1 | async-start | bytes 32768 | tf_op jit(solution)/shard_map/all_to_all | solution.py:69
  23.2 7.2 %collective-permute-start.2 = (bf16[4,8,256]{2,1,0:T(8,128)(2,1)S(1)}, bf16[4,8,256]{2,1,0:T(8,128)(2,1)S(1)}, u32[]{:S(2)}, u32[]{:S(2)}) collective-permute-start(bf16[4,8,256]{2,1,0:T(8,128)(2,1)S(1)} %pad_maximum_fusion.2), channel_id=1, source_target_pairs={{0,4},{1,5},{2,6},{3,7},{4,0},{5,1},{6,2},{7,3},{8,12},{9,13},{10,... | collective-permute-start | bytes 49160 | tf_op jit(solution)/shard_map/ppermute | solution.py:19
  30.4 14.6 %collective-permute-start.3 = (bf16[8,8,256]{2,1,0:T(8,128)(2,1)S(1)}, bf16[8,8,256]{2,1,0:T(8,128)(2,1)S(1)}, u32[]{:S(2)}, u32[]{:S(2)}) collective-permute-start(bf16[8,8,256]{2,1,0:T(8,128)(2,1)S(1)} %pad_maximum_fusion.1), channel_id=1, source_target_pairs={{0,8},{1,9},{2,10},{3,11},{4,12},{5,13},{6,14},{7,15},{8,0},{9,1},... | collective-permute-start | bytes 98312 | tf_op jit(solution)/shard_map/ppermute | solution.py:19
  42.4 199.2 %all-to-all-start.1 = ((bf16[32,8,2048]{2,1,0:T(8,128)(2,1)}), bf16[32,8,2048]{2,1,0:T(8,128)(2,1)S(1)}, u32[]{:S(2)}, u32[]{:S(2)}) async-start(bf16[32,8,2048]{2,1,0:T(8,128)(2,1)} %bitcast.7), calls=%async_computation.2 | async-start | bytes 2097152 | tf_op jit(solution)/shard_map/all_to_all | solution.py:67
  45.0 195.2 %reduce-scatter.2.cloned.1.call-start = ((), (), s32[]{:S(2)}) async-start(), calls=%async_computation.3 | async-start | bytes 270336 | tf_op jit(solution)/shard_map/reduce_scatter | solution.py:52
  45.1 11.3 %collective-permute-start.4 = (bf16[16,8,256]{2,1,0:T(8,128)(2,1)S(1)}, bf16[16,8,256]{2,1,0:T(8,128)(2,1)S(1)}, u32[]{:S(2)}, u32[]{:S(2)}) collective-permute-start(bf16[16,8,256]{2,1,0:T(8,128)(2,1)S(1)} %pad_maximum_fusion), channel_id=1, source_target_pairs={{0,16},{1,17},{2,18},{3,19},{4,20},{5,21},{6,22},{7,23},{8,24},{9,... | collective-permute-start | bytes 196616 | tf_op jit(solution)/shard_map/ppermute | solution.py:19
  147.7 95.6 %copy-start = (f32[8]{0:T(128)}, f32[8]{0:T(128)S(1)}, u32[]{:S(2)}) copy-start(f32[8]{0:T(128)S(1)} %get-tuple-element.3) | copy-start | bytes 100
  241.5 1.4 copy-start.1
Sparse Core Ops, SparseCore 0:
  104.2 135.9 reduce-scatter.1
